TPU v7x, 256 devices: a whole 4x4x8 slice. The times are simulated.
256 devices in a mesh: facet: 16 (over y, x_hi, core), bl: 16 (over z, x_lo).
Axes of the slice: x: 4 (x_hi: 2, x_lo: 2; x = x_hi * 2 + x_lo), y: 4, z: 8, core: 2. Of those that a mesh axis runs over, the one named last changes fastest.
Arguments:
- facet_model: bfloat16 [16, 1024, 1024], P('facet', 'bl'), may hold values from -0.005859375 to 0.005859375
- screens: bfloat16 [16, 256, 64, 128], P('facet', 'bl'), may hold values from 0.099609375 to 1.8984375
- observed: float32 [192, 64, 128], P('bl'), may hold values from -24 to 24
- offsets: int32 [192, 2], P('bl'), may hold values from 0 to 4032
- stations: int32 [192, 2], P('bl'), may hold values from 0 to 255
- counts: int32 [16], P('bl'), may hold values from 1 to 12, as said below
Outputs:
- residual_vis: float32 [192, 64, 128], P('bl')
- residual_image: float32 [16, 1024, 1024], P('facet', 'bl')
Inputs may be any that keep to these rules, and one draw needn't show every extreme that they name: `counts`: some baseline block has all 12 slots live.
All inputs are finite; a program needn't handle non-finite values.
Results may differ from a plain program's by a relative error of at most 0.0061.
Values may be sent and summed in bfloat16 or wider, within the bound.
No kernel may reach another device: no remote copies, remote signals or barrier semaphores. Data moves between devices by JAX's collectives and lax.ppermute only.
A program may use at most 64 MiB of HBM per device.

v0:
```python
import math
import jax
import jax.numpy as jnp
from jax import lax
from jax.sharding import PartitionSpec as P

FGRID = 4


def tables(offset_u, offset_v, facet_id, tile_width, facet_cells):
    grid_cells = FGRID * facet_cells
    corner_x = facet_id // FGRID * facet_cells
    corner_y = facet_id % FGRID * facet_cells
    pixel_index = jnp.arange(facet_cells, dtype=jnp.int32)
    cell_index = jnp.arange(tile_width, dtype=jnp.int32)
    phase_u = jnp.mod(
        (offset_u + cell_index)[:, None] * (corner_x + pixel_index)[None, :], grid_cells
    )
    phase_v = jnp.mod(
        (offset_v + cell_index)[:, None] * (corner_y + pixel_index)[None, :], grid_cells
    )
    angle_u = phase_u.astype(jnp.float32) * (2.0 * math.pi / grid_cells)
    angle_v = phase_v.astype(jnp.float32) * (2.0 * math.pi / grid_cells)
    tab_u = jnp.concatenate([jnp.cos(angle_u), -jnp.sin(angle_u)], axis=0).astype(jnp.bfloat16)
    table_vertical = jnp.concatenate([jnp.cos(angle_v), jnp.sin(angle_v)], axis=0).astype(
        jnp.bfloat16
    )
    return (tab_u, table_vertical)


def half_splits(value):
    half_width = value.shape[-1] // 2
    return (value[..., :half_width], value[..., half_width:])


def complex_times(left_re, left_im, right_re, right_im):
    return (left_re * right_re - left_im * right_im, left_re * right_im + left_im * right_re)


def times_conj(left_re, left_im, right_re, right_im):
    return (left_re * right_re + left_im * right_im, left_im * right_re - left_re * right_im)


def per_device(facet_model, screens, observed, offsets, stations, counts):
    tile_count = observed.shape[0]
    tile_width = observed.shape[1]
    facet_cells = facet_model.shape[2]
    bl_devices = lax.axis_size("bl")
    facet_id = lax.axis_index("facet")
    make_tables = jax.vmap(tables, in_axes=(0, 0, None, None, None))
    tab_u, table_vertical = make_tables(
        offsets[:, 0], offsets[:, 1], facet_id, tile_width, facet_cells
    )
    upper_portion = jnp.einsum(
        "tkn,np->tkp",
        tab_u,
        lax.all_gather(facet_model[0], "bl", axis=0, tiled=True),
        preferred_element_type=jnp.float32,
    ).astype(jnp.bfloat16)
    block_groups = jnp.einsum(
        "gsf,gmf->gsm", upper_portion, table_vertical, preferred_element_type=jnp.float32
    )
    real_part = (
        block_groups[:, :tile_width, :tile_width] + block_groups[:, tile_width:, tile_width:]
    )
    imag_part = (
        block_groups[:, tile_width:, :tile_width] - block_groups[:, :tile_width, tile_width:]
    )
    all_screens = lax.all_gather(screens[0], "bl", axis=0, tiled=True)
    first_station_gain = jnp.take(all_screens, stations[:, 0], axis=0).astype(jnp.float32)
    gain_q = jnp.take(all_screens, stations[:, 1], axis=0).astype(jnp.float32)
    p_re, p_im = half_splits(first_station_gain)
    q_re, q_im = half_splits(gain_q)
    y_re, y_im = complex_times(p_re, p_im, real_part, imag_part)
    x_re, x_im = times_conj(y_re, y_im, q_re, q_im)
    contribution = jnp.concatenate([x_re, x_im], axis=2)
    live_mask = (jnp.arange(tile_count, dtype=jnp.int32) < counts[0])[:, None, None]
    predicted = lax.psum(contribution, "facet")
    residual = jnp.where(live_mask, observed - predicted, jnp.zeros_like(observed))
    r_re, r_im = half_splits(residual)
    z_re, z_im = times_conj(r_re, r_im, p_re, p_im)
    w_re, w_im = complex_times(z_re, z_im, q_re, q_im)
    w_re = w_re.astype(jnp.bfloat16)
    w_im = w_im.astype(jnp.bfloat16)
    stacked = jnp.concatenate(
        [jnp.concatenate([w_re, -w_im], axis=2), jnp.concatenate([w_im, w_re], axis=2)], axis=1
    )
    q_two = jnp.einsum(
        "tuk,tky->tuy", stacked, table_vertical, preferred_element_type=jnp.float32
    ).astype(jnp.bfloat16)
    image_scale = 1.0 / (32.0 * tile_width * math.sqrt(tile_count * bl_devices))
    row_count = facet_cells // bl_devices
    whole_image = jnp.einsum("tkx,tky->xy", tab_u, q_two, preferred_element_type=jnp.float32)
    summed = lax.psum(whole_image, "bl")
    own_rows = lax.dynamic_slice_in_dim(summed, lax.axis_index("bl") * row_count, row_count, 0)
    residual_image = (own_rows * image_scale)[None]
    return (residual, residual_image)


def solution(mesh):
    in_specs = (
        P("facet", "bl", None),
        P("facet", "bl", None, None),
        P("bl", None, None),
        P("bl", None),
        P("bl", None),
        P("bl"),
    )
    out_specs = (P("bl", None, None), P("facet", "bl", None))
    return jax.shard_map(
        per_device, mesh=mesh, in_specs=in_specs, out_specs=out_specs, check_vma=False
    )
```

profile of v0, /device:TPU:16, one launch (start us, length us, event | category | flops | bytes accessed | tf_op | source)
XLA Modules:
  0.0 557.0 jit_solution(6302353294279317188)
XLA Ops:
  7.2 0.0 all-gather.7.cloned.1.call-start
  7.2 0.7 all-gather.7.cloned.1.call-update
  7.9 0.0 all-gather.5.cloned.1.call-start
  7.9 0.7 all-gather.5.cloned.1.call-update
  8.6 0.0 all-reduce.3.cloned.1.call-start
  8.7 0.8 compare_and_fusion.1
  9.5 0.8 slice_bitcast_fusion.1
  10.3 0.1 iota_add_fusion
  10.4 14.1 %cosine_convert_fusion = (bf16[12,64,1024]{2,1,0:T(8,128)(2,1)S(1)}, bf16[12,64,1024]{2,1,0:T(8,128)(2,1)}) fusion(s32[1024]{0:T(1024)S(1)} %iota_add_fusion.2, s32[12,64]{1,0:T(8,128)S(1)} %get-tuple-element.24), kind=kLoop, calls=%fused_computation.23 | loop fusion | flops 12582912 | bytes 3152896 | tf_op jit(solution)/shard_map/convert
  24.4 14.2 %cosine_convert_fusion.1 = (bf16[12,64,1024]{2,1,0:T(8,128)(2,1)}, bf16[12,64,1024]{2,1,0:T(8,128)(2,1)}) fusion(s32[1024]{0:T(1024)S(1)} %iota_add_fusion.3, s32[12,64]{1,0:T(8,128)S(1)} %get-tuple-element.25), kind=kLoop, calls=%fused_computation.27 | loop fusion | flops 13369344 | bytes 3152896 | tf_op jit(solution)/shard_map/convert.2
  38.7 46.7 %all-gather.7.cloned.1.call-done = bf16[1,1024,1024]{2,1,0:T(8,128)(2,1)} async-done(((bf16[1,64,1024]{2,1,0:T(8,128)(2,1)}), bf16[1,1024,1024]{2,1,0:T(8,128)(2,1)}) %all-gather.7.cloned.1.call-update) | async-done | bytes 2097168 | tf_op jit(solution)/shard_map/all_gather | solution.py:57
  85.4 7.2 %fusion.8 = f32[12,128,128]{2,1,0:T(8,128)S(1)} fusion(bf16[12,64,1024]{2,1,0:T(8,128)(2,1)} %get-tuple-element.17, bf16[12,64,1024]{2,1,0:T(8,128)(2,1)S(1)} %get-tuple-element.16, bf16[1,1024,1024]{2,1,0:T(8,128)(2,1)} %all-gather.7.cloned.1.call-done, bf16[12,64,1024]{2,1,0:T(8,128)(2,1)} %get-tuple-element.15, bf16[12,64,1024]{2,1,0:T(8,128)(2,1)} %get-tuple-element.14), kind=kOutput, calls=%fused_computation.24 | convolution fusion | flops 3638034432 | bytes 9175040 | tf_op jit(solution)/shard_map/gsf,gmf->gsm/dot_general | solution.py:60
  92.6 92.0 %all-gather.5.cloned.1.call-done = bf16[1,256,64,128]{3,2,0,1:T(8,128)(2,1)} async-done(((bf16[1,16,64,128]{3,2,0,1:T(8,128)(2,1)}), bf16[1,256,64,128]{3,2,0,1:T(8,128)(2,1)}) %all-gather.5.cloned.1.call-update) | async-done | bytes 4194320 | tf_op jit(solution)/shard_map/all_gather | solution.py:69
  184.6 2.8 gather_fusion.1
  187.4 2.8 gather_fusion
  190.1 0.1 select_convert_fusion
  190.3 0.0 copy-start.1
  190.3 0.5 multiply_add_fusion.1
  190.8 0.2 multiply_subtract_fusion.1
  191.0 0.9 pad_maximum_fusion.11
  191.9 0.0 all-reduce.3.cloned.1.call-update
  191.9 0.2 all-reduce.5.cloned.1.call-start
  192.8 134.5 %all-reduce.3.cloned.1.call-done = f32[12,64,128]{2,1,0:T(8,128)} async-done(((f32[12,64,128]{2,1,0:T(8,128)}), f32[12,64,128]{2,1,0:T(8,128)}) %all-reduce.3.cloned.1.call-update) | async-done | bytes 393232 | tf_op jit(solution)/shard_map/psum | solution.py:78
  327.3 0.0 copy-done.1
  327.3 1.1 subtract_select_fusion
  328.4 0.0 copy-start
  328.4 0.4 fusion.39
  328.8 0.2 subtract_convert_fusion
  329.0 8.6 %fusion.12 = f32[1024,1024]{1,0:T(8,128)} fusion(bf16[12,64,1024]{2,1,0:T(8,128)(2,1)} %get-tuple-element.17, bf16[12,64,1024]{2,1,0:T(8,128)(2,1)S(1)} %get-tuple-element.16, bf16[12,64,1024]{2,1,0:T(8,128)(2,1)} %get-tuple-element.15, bf16[12,64,1024]{2,1,0:T(8,128)(2,1)} %get-tuple-element.14, bf16[12,64,64]{2,1,0:T(8,128)(2,1)S(1)} %subtract_convert_fusion, ...), kind=kOutput, calls=%fused_computation.29 | convolution fusion | flops 3639607296 | bytes 10780672 | tf_op jit(solution)/shard_map/tkx,tky->xy/dot_general | solution.py:93
  337.6 0.0 copy-done
  337.6 0.0 all-reduce.5.cloned.1.call-update
  337.7 211.1 %all-reduce.5.cloned.1.call-done = f32[1024,1024]{1,0:T(8,128)} async-done(((f32[1024,1024]{1,0:T(8,128)}), f32[1024,1024]{1,0:T(8,128)}) %all-reduce.5.cloned.1.call-update) | async-done | bytes 4194320 | tf_op jit(solution)/shard_map/psum | solution.py:94
  548.8 1.7 multiply_bitcast_fusion
  (5 shorter events, 0.0 us)
Async XLA Ops:
  7.2 78.2 %all-gather.7.cloned.1.call-start = ((), (), s32[]{:S(2)}) async-start(), calls=%async_computation.3 | async-start | bytes 2228224 | tf_op jit(solution)/shard_map/all_gather | solution.py:57
  7.9 176.7 %all-gather.5.cloned.1.call-start = ((), (), s32[]{:S(2)}) async-start(), calls=%async_computation.2 | async-start | bytes 4456448 | tf_op jit(solution)/shard_map/all_gather | solution.py:69
  8.6 318.6 %all-reduce.3.cloned.1.call-start = ((), (), s32[]{:S(2)}) async-start(), calls=%async_computation | async-start | bytes 786432 | tf_op jit(solution)/shard_map/psum | solution.py:78
  190.3 137.0 %copy-start.1 = (f32[12,64,128]{2,1,0:T(8,128)S(1)}, f32[12,64,128]{2,1,0:T(8,128)}, u32[]{:S(2)}) copy-start(f32[12,64,128]{2,1,0:T(8,128)} %param.10) | copy-start | bytes 1179652
  191.9 356.9 %all-reduce.5.cloned.1.call-start = ((), (), s32[]{:S(2)}) async-start(), calls=%async_computation.1 | async-start | bytes 8388608 | tf_op jit(solution)/shard_map/psum | solution.py:94
  328.4 9.2 %copy-start = (f32[12,64,128]{2,1,0:T(8,128)}, f32[12,64,128]{2,1,0:T(8,128)S(1)}, u32[]{:S(2)}) copy-start(f32[12,64,128]{2,1,0:T(8,128)S(1)} %subtract_select_fusion) | copy-start | bytes 1179652
Sparse Core Ops, SparseCore 0:
  9.8 75.5 all-gather.6
  87.2 97.3 all-gather.4
  192.0 135.2 all-reduce.2
  337.8 210.9 all-reduce.4
where the time goes:
time: 557 us
  waiting for transfers between devices  486 us (87%)
  other arithmetic  34.2 us (6%)
  matrix products  15.9 us (3%)
  between operations  14.6 us (3%)
  local copies, waits for them, and re-layouts  6.31 us (1%)
    psum x1, waiting for transfers between devices, per_device(): summed = lax.psum(whole_image, 'bl')  211 us
    psum x1, waiting for transfers between devices, per_device(): predicted = lax.psum(contribution, 'facet')  134 us
    all_gather x1, waiting for transfers between devices, per_device(): all_screens = lax.all_gather(screens[0], 'bl', axis=0, tiled=True)  92 us
    all_gather x1, waiting for transfers between devices, per_device(): lax.all_gather(facet_model[0], 'bl', axis=0, tiled=True)  46.7 us
    another operation x2, other arithmetic  28.3 us
  transfers between devices with their start and end apart: 4, of which 4 were waited for; matrix products, arithmetic and copies ran while one was open for 7% of the time, Pallas kernels for 0%

commit v1 on v0

--- a/solution.py
+++ b/solution.py
@@ -75,7 +75,8 @@
     x_re, x_im = times_conj(y_re, y_im, q_re, q_im)
     contribution = jnp.concatenate([x_re, x_im], axis=2)
     live_mask = (jnp.arange(tile_count, dtype=jnp.int32) < counts[0])[:, None, None]
-    predicted = lax.psum(contribution, "facet")
+    parts = lax.all_gather(contribution, "facet")
+    predicted = jnp.sum(parts, axis=0)
     residual = jnp.where(live_mask, observed - predicted, jnp.zeros_like(observed))
     r_re, r_im = half_splits(residual)
     z_re, z_im = times_conj(r_re, r_im, p_re, p_im)

time: 557 us -> 480 us (0.86)
  waiting for transfers between devices: 486 us -> 407 us
    psum x1 -> x0, waiting for transfers between devices: 134 us -> none  [per_device(): predicted = lax.psum(contribution, 'facet')]
    all_gather x0 -> x1, waiting for transfers between devices: none -> 66 us  [per_device(): parts = lax.all_gather(contribution, 'facet')]
    psum x1, waiting for transfers between devices: 211 us -> 200 us  [per_device(): summed = lax.psum(whole_image, 'bl')]
  transfers between devices with their start and end apart: 4 -> 4, of which waited for: 4 -> 4; matrix products, arithmetic and copies ran while one was open for 7% -> 8% of each run, Pallas kernels for 0% -> 0%
where the time goes in v1:
time: 480 us
  waiting for transfers between devices  407 us (85%)
  other arithmetic  36.6 us (8%)
  matrix products  15.9 us (3%)
  between operations  14.6 us (3%)
  local copies, waits for them, and re-layouts  6.31 us (1%)
    psum x1, waiting for transfers between devices, per_device(): summed = lax.psum(whole_image, 'bl')  200 us
    all_gather x1, waiting for transfers between devices, per_device(): all_screens = lax.all_gather(screens[0], 'bl', axis=0, tiled=True)  92 us
    all_gather x1, waiting for transfers between devices, per_device(): parts = lax.all_gather(contribution, 'facet')  66 us
    all_gather x1, waiting for transfers between devices, per_device(): lax.all_gather(facet_model[0], 'bl', axis=0, tiled=True)  46.7 us
    another operation x2, other arithmetic  28.3 us
  transfers between devices with their start and end apart: 4, of which 4 were waited for; matrix products, arithmetic and copies ran while one was open for 8% of the time, Pallas kernels for 0%

profile of v1, /device:TPU:16, one launch (start us, length us, event | category | flops | bytes accessed | tf_op | source)
XLA Modules:
  0.0 480.3 jit_solution(14527273502621721568)
XLA Ops:
  7.2 0.0 all-gather.9.cloned.1.call-start
  7.2 0.7 all-gather.9.cloned.1.call-update
  7.9 0.0 all-gather.7.cloned.1.call-start
  7.9 0.7 all-gather.7.cloned.1.call-update
  8.6 0.0 all-gather.11.cloned.1.call-start
  8.7 0.8 compare_and_fusion.1
  9.5 0.8 slice_bitcast_fusion.1
  10.3 0.1 iota_add_fusion
  10.4 14.1 %cosine_convert_fusion = (bf16[12,64,1024]{2,1,0:T(8,128)(2,1)S(1)}, bf16[12,64,1024]{2,1,0:T(8,128)(2,1)}) fusion(s32[1024]{0:T(1024)S(1)} %iota_add_fusion.2, s32[12,64]{1,0:T(8,128)S(1)} %get-tuple-element.24), kind=kLoop, calls=%fused_computation.23 | loop fusion | flops 12582912 | bytes 3152896 | tf_op jit(solution)/shard_map/convert
  24.4 14.2 %cosine_convert_fusion.1 = (bf16[12,64,1024]{2,1,0:T(8,128)(2,1)}, bf16[12,64,1024]{2,1,0:T(8,128)(2,1)}) fusion(s32[1024]{0:T(1024)S(1)} %iota_add_fusion.3, s32[12,64]{1,0:T(8,128)S(1)} %get-tuple-element.25), kind=kLoop, calls=%fused_computation.27 | loop fusion | flops 13369344 | bytes 3152896 | tf_op jit(solution)/shard_map/convert.2
  38.7 46.7 %all-gather.9.cloned.1.call-done = bf16[1,1024,1024]{2,1,0:T(8,128)(2,1)} async-done(((bf16[1,64,1024]{2,1,0:T(8,128)(2,1)}), bf16[1,1024,1024]{2,1,0:T(8,128)(2,1)}) %all-gather.9.cloned.1.call-update) | async-done | bytes 2097168 | tf_op jit(solution)/shard_map/all_gather | solution.py:57
  85.4 7.2 %fusion.8 = f32[12,128,128]{2,1,0:T(8,128)S(1)} fusion(bf16[12,64,1024]{2,1,0:T(8,128)(2,1)} %get-tuple-element.17, bf16[12,64,1024]{2,1,0:T(8,128)(2,1)S(1)} %get-tuple-element.16, bf16[1,1024,1024]{2,1,0:T(8,128)(2,1)} %all-gather.9.cloned.1.call-done, bf16[12,64,1024]{2,1,0:T(8,128)(2,1)} %get-tuple-element.15, bf16[12,64,1024]{2,1,0:T(8,128)(2,1)} %get-tuple-element.14), kind=kOutput, calls=%fused_computation.24 | convolution fusion | flops 3638034432 | bytes 9175040 | tf_op jit(solution)/shard_map/gsf,gmf->gsm/dot_general | solution.py:60
  92.6 92.0 %all-gather.7.cloned.1.call-done = bf16[1,256,64,128]{3,2,0,1:T(8,128)(2,1)} async-done(((bf16[1,16,64,128]{3,2,0,1:T(8,128)(2,1)}), bf16[1,256,64,128]{3,2,0,1:T(8,128)(2,1)}) %all-gather.7.cloned.1.call-update) | async-done | bytes 4194320 | tf_op jit(solution)/shard_map/all_gather | solution.py:69
  184.6 2.8 gather_fusion
  187.4 2.8 gather_fusion.1
  190.1 0.1 select_convert_fusion
  190.3 0.5 multiply_add_fusion.1
  190.8 0.2 multiply_subtract_fusion.1
  190.9 0.9 pad_maximum_fusion.11
  191.9 0.0 all-gather.11.cloned.1.call-update
  191.9 0.2 all-reduce.2.cloned.1.call-start
  192.8 66.0 %all-gather.11.cloned.1.call-done = f32[192,64,128]{2,1,0:T(8,128)} async-done(((f32[12,64,128]{2,1,0:T(8,128)}), f32[192,64,128]{2,1,0:T(8,128)}) %all-gather.11.cloned.1.call-update) | async-done | bytes 6291472 | tf_op jit(solution)/shard_map/all_gather | solution.py:78
  258.8 0.0 copy-start.1
  258.8 3.4 reduce_sum.9
  262.2 0.0 copy-done.1
  262.2 0.1 subtract_select_fusion
  262.3 0.0 copy-start
  262.3 0.4 fusion.39
  262.7 0.2 subtract_convert_fusion
  262.9 8.7 %fusion.12 = f32[1024,1024]{1,0:T(8,128)} fusion(bf16[12,64,1024]{2,1,0:T(8,128)(2,1)} %get-tuple-element.17, bf16[12,64,1024]{2,1,0:T(8,128)(2,1)S(1)} %get-tuple-element.16, bf16[12,64,1024]{2,1,0:T(8,128)(2,1)} %get-tuple-element.15, bf16[12,64,1024]{2,1,0:T(8,128)(2,1)} %get-tuple-element.14, bf16[12,64,64]{2,1,0:T(8,128)(2,1)S(1)} %subtract_convert_fusion, ...), kind=kOutput, calls=%fused_computation.29 | convolution fusion | flops 3639607296 | bytes 10780672 | tf_op jit(solution)/shard_map/tkx,tky->xy/dot_general | solution.py:94
  271.6 0.0 copy-done
  271.6 0.0 all-reduce.2.cloned.1.call-update
  271.6 200.5 %all-reduce.2.cloned.1.call-done = f32[1024,1024]{1,0:T(8,128)} async-done(((f32[1024,1024]{1,0:T(8,128)}), f32[1024,1024]{1,0:T(8,128)}) %all-reduce.2.cloned.1.call-update) | async-done | bytes 4194320 | tf_op jit(solution)/shard_map/psum | solution.py:95
  472.1 1.7 multiply_bitcast_fusion
  (5 shorter events, 0.0 us)
Async XLA Ops:
  7.2 78.2 %all-gather.9.cloned.1.call-start = ((), (), s32[]{:S(2)}) async-start(), calls=%async_computation.2 | async-start | bytes 2228224 | tf_op jit(solution)/shard_map/all_gather | solution.py:57
  7.9 176.7 %all-gather.7.cloned.1.call-start = ((), (), s32[]{:S(2)}) async-start(), calls=%async_computation.1 | async-start | bytes 4456448 | tf_op jit(solution)/shard_map/all_gather | solution.py:69
  8.6 250.1 %all-gather.11.cloned.1.call-start = ((), (), s32[]{:S(2)}) async-start(), calls=%async_computation.3 | async-start | bytes 6684672 | tf_op jit(solution)/shard_map/all_gather | solution.py:78
  191.9 280.2 %all-reduce.2.cloned.1.call-start = ((), (), s32[]{:S(2)}) async-start(), calls=%async_computation | async-start | bytes 8388608 | tf_op jit(solution)/shard_map/psum | solution.py:95
  258.8 3.4 copy-start.1
  262.3 9.3 %copy-start = (f32[12,64,128]{2,1,0:T(8,128)}, f32[12,64,128]{2,1,0:T(8,128)S(1)}, u32[]{:S(2)}) copy-start(f32[12,64,128]{2,1,0:T(8,128)S(1)} %subtract_select_fusion) | copy-start | bytes 1179652
Sparse Core Ops, SparseCore 0:
  9.8 75.5 all-gather.8
  87.2 97.3 all-gather.6
  192.0 66.7 all-gather.10
  271.7 200.2 all-reduce.1
